TPU v7x, 32 devices: a whole 2x2x4 slice. The times are simulated.
32 devices in a mesh: dp: 8 (over z, y), tensor: 4 (over x, core).
Axes of the slice: x: 2, y: 2, z: 4, core: 2. Of those that a mesh axis runs over, the one named last changes fastest.
Arguments:
- inputs: bfloat16 [1024, 3200], P('dp'), may hold values from -6 to 6
- norm_gain: float32 [3200], replicated, may hold values from 0.25 to 1.75
- fc1_weight: bfloat16 [3200, 8192], P(None, 'tensor'), may hold values from -0.109375 to 0.109375
- fc1_bias: float32 [8192], P('tensor'), may hold values from -4 to 4
- grad_act: bfloat16 [1024, 8192], P('dp', 'tensor'), may hold values from -6 to 6
- grad_res: bfloat16 [1024, 3200], P(('dp', 'tensor')), may hold values from -6 to 6
Outputs:
- grad_inputs: bfloat16 [1024, 3200], P(('dp', 'tensor'))
- grad_weight: float32 [3200, 8192], P('dp', 'tensor')
- grad_bias: float32 [8192], P('tensor')
- grad_gain: float32 [3200], replicated
All inputs are finite; a program needn't handle non-finite values.
Results may differ from a plain program's by a relative error of at most 0.008.
Values may be sent and summed in bfloat16 or wider, within the bound.
No kernel may reach another device: no remote copies, remote signals or barrier semaphores. Data moves between devices by JAX's collectives and lax.ppermute only.
A program may use at most 192 MiB of HBM per device.

v0:
```python
import jax
import jax.numpy as jnp
from jax import lax
from jax.sharding import PartitionSpec as P

epsilon = 1e-06


def on_device(inputs, norm_gain, fc1_weight, fc1_bias, grad_act, grad_res):
    dp_size = lax.axis_size("dp")
    tensor_size = lax.axis_size("tensor")
    tokens, width = inputs.shape
    owner_rows = width // dp_size
    values = inputs.astype(jnp.float32)
    inverse = lax.rsqrt(jnp.mean(values * values, axis=-1, keepdims=True) + epsilon)
    normalized = values * inverse
    normed = (normalized * norm_gain).astype(jnp.bfloat16)
    blocks = normed.reshape(tokens, dp_size, owner_rows).transpose(1, 0, 2)
    owned_cols = lax.all_to_all(blocks, "dp", 0, 0, tiled=True).reshape(
        dp_size * tokens, owner_rows
    )
    preact = jnp.dot(normed, fc1_weight, preferred_element_type=jnp.float32) + fc1_bias
    derivative = (
        0.5 * (1.0 + lax.erf(preact * 0.7071067811865476))
        + preact * jnp.exp(-0.5 * preact * preact) * 0.3989422804014327
    )
    grad_pre = (grad_act.astype(jnp.float32) * derivative).astype(jnp.bfloat16)
    grad_pre_all = lax.all_gather(grad_pre, "dp", axis=0, tiled=True)
    back_term = lax.dot_general(
        grad_pre, fc1_weight, (((1,), (1,)), ((), ())), preferred_element_type=jnp.float32
    )
    dnormed = lax.psum_scatter(
        back_term.astype(jnp.bfloat16), "tensor", scatter_dimension=0, tiled=True
    ).astype(jnp.float32)
    grad_weight = lax.dot_general(
        owned_cols, grad_pre_all, (((0,), (0,)), ((), ())), preferred_element_type=jnp.float32
    )
    grad_bias = jnp.sum(grad_pre_all.astype(jnp.float32), axis=0)
    row_count = tokens // tensor_size
    row_start = lax.axis_index("tensor") * row_count
    normalized_rows = lax.dynamic_slice_in_dim(normalized, row_start, row_count, 0)
    inverse_rows = lax.dynamic_slice_in_dim(inverse, row_start, row_count, 0)
    gain_part = jnp.sum(dnormed * normalized_rows, axis=0)
    grad_hat = dnormed * norm_gain
    projection = jnp.mean(grad_hat * normalized_rows, axis=-1, keepdims=True)
    grad_inputs = (
        grad_res.astype(jnp.float32) + inverse_rows * (grad_hat - normalized_rows * projection)
    ).astype(jnp.bfloat16)
    grad_gain = lax.psum(gain_part, ("dp", "tensor"))
    return (grad_inputs, grad_weight, grad_bias, grad_gain)


def solution(mesh):
    in_specs = (
        P("dp", None),
        P(),
        P(None, "tensor"),
        P("tensor"),
        P("dp", "tensor"),
        P(("dp", "tensor"), None),
    )
    out_specs = (P(("dp", "tensor"), None), P("dp", "tensor"), P("tensor"), P())
    return jax.shard_map(
        on_device, mesh=mesh, in_specs=in_specs, out_specs=out_specs, check_vma=False
    )
```

profile of v0, /device:TPU:0, one launch (start us, length us, event | category | flops | bytes accessed | tf_op | source)
XLA Modules:
  0.0 137.2 jit_solution(2387657877034527978)
XLA Ops:
  8.0 0.0 copy-start
  8.0 0.0 reduce-scatter.2.cloned.1.call-start
  8.1 1.4 %fusion = f32[128]{0:T(128)S(1)} fusion(bf16[128,3200]{1,0:T(8,128)(2,1)} %param.6), kind=kLoop, calls=%fused_computation.5 | loop fusion | flops 1228672 | bytes 819712 | tf_op jit(solution)/shard_map/reduce_sum | solution.py:15
  9.5 1.4 %convert_multiply_fusion = (f32[128,3200]{1,0:T(8,128)S(1)}, bf16[128,3200]{1,0:T(8,128)(2,1)S(1)}) fusion(bf16[128,3200]{1,0:T(8,128)(2,1)} %param.6, f32[128]{0:T(128)S(1)} %add_rsqrt_fusion, f32[3200]{0:T(1024)} %param.7), kind=kLoop, calls=%fused_computation.3 | loop fusion | flops 1638400 | bytes 3290112 | tf_op jit(solution)/shard_map/mul | solution.py:16
  10.9 0.0 copy-done
  10.9 8.0 %fusion.6 = (bf16[128,2048]{1,0:T(8,128)(2,1)}, f32[128,2048]{1,0:T(8,128)S(1)}) fusion(bf16[128,2048]{1,0:T(8,128)(2,1)S(1)} %copy-done, f32[2048]{0:T(1024)} %param.9, bf16[128,3200]{1,0:T(8,128)(2,1)S(1)} %get-tuple-element.7, bf16[3200,2048]{1,0:T(8,128)(2,1)} %param.8), kind=kOutput, calls=%fused_computation.13 | convolution fusion | flops 1680867328 | bytes 16031744 | tf_op jit(solution)/shard_map/dot_general | solution.py:22
  18.9 10.0 %convolution_convert_fusion = bf16[128,3200]{1,0:T(8,128)(2,1)} fusion(bf16[3200,2048]{1,0:T(8,128)(2,1)} %param.8, f32[128,2048]{1,0:T(8,128)S(1)} %get-tuple-element.9, bf16[128,2048]{1,0:T(8,128)(2,1)S(1)} %copy-done), kind=kOutput, calls=%fused_computation.1 | convolution fusion | flops 1681014784 | bytes 15499264 | tf_op jit(solution)/shard_map/dot_general | solution.py:29
  28.9 0.0 copy-start.2
  28.9 0.0 copy-start.1
  28.9 0.0 reduce-scatter.2.cloned.1.call-update
  29.0 0.0 all-gather.2.cloned.1.call-start
  29.0 0.5 all-gather.2.cloned.1.call-update
  29.5 1.3 copy.10
  30.8 7.3 %all-to-all-start = ((bf16[8,128,400]{1,2,0:T(8,128)(2,1)}), bf16[8,128,400]{1,2,0:T(8,128)(2,1)S(1)}, u32[]{:S(2)}, u32[]{:S(2)}) async-start(bf16[8,128,400]{1,2,0:T(8,128)(2,1)} %bitcast.1), calls=%async_computation.1 | async-start | bytes 1638400 | tf_op jit(solution)/shard_map/all_to_all | solution.py:19
  38.2 0.1 dynamic-slice.3
  38.2 17.0 %reduce-scatter.2.cloned.1.call-done = bf16[32,3200]{1,0:T(8,128)(2,1)} async-done(((bf16[128,3200]{1,0:T(8,128)(2,1)}), bf16[32,3200]{1,0:T(8,128)(2,1)}) %reduce-scatter.2.cloned.1.call-update) | async-done | bytes 204816 | tf_op jit(solution)/shard_map/reduce_scatter | solution.py:32
  55.3 0.0 copy-done.2
  55.3 1.1 fusion.23
  56.4 41.7 %psum.7 = f32[3200]{0:T(1024)} all-reduce(f32[3200]{0:T(1024)S(1)} %get-tuple-element.4), channel_id=1, replica_groups=mesh['dp'=8,'tensor'=4] {'dp','tensor'}, use_global_device_ids=true, to_apply=%region_5.0 | all-reduce | flops 3200 | bytes 25600 | tf_op jit(solution)/shard_map/psum | solution.py:49
  98.1 0.0 copy-done.1
  98.1 1.8 %fusion.22 = bf16[32,3200]{1,0:T(8,128)(2,1)} fusion(bf16[32,3200]{1,0:T(8,128)(2,1)} %reduce-scatter.2.cloned.1.call-done, bf16[32,3200]{1,0:T(8,128)(2,1)S(1)} %copy-done.1, f32[128,3200]{1,0:T(8,128)S(1)} %get-tuple-element.6, s32[]{:T(128)S(6)} %select_n.4, f32[32]{0:T(128)S(1)} %broadcast_multiply_fusion, f32[3200]{0:T(1024)S(1)} %copy-done.2, ...), kind=kLoop, calls=%fused_computation.30 | loop fusion | flops 819200 | bytes 1037060 | tf_op jit(solution)/shard_map/convert_element_type | solution.py:48
  99.9 20.6 %all-gather.2.cloned.1.call-done = bf16[1024,2048]{1,0:T(8,128)(2,1)} async-done(((bf16[128,2048]{1,0:T(8,128)(2,1)}), bf16[1024,2048]{1,0:T(8,128)(2,1)}) %all-gather.2.cloned.1.call-update) | async-done | bytes 4194320 | tf_op jit(solution)/shard_map/all_gather | solution.py:28
  120.5 3.4 %convert_reduce_fusion = f32[2048]{0:T(1024)} fusion(bf16[1024,2048]{1,0:T(8,128)(2,1)} %all-gather.2.cloned.1.call-done), kind=kLoop, calls=%fused_computation | loop fusion | flops 4192256 | bytes 4202496 | tf_op jit(solution)/shard_map/reduce_sum | solution.py:38
  124.0 0.0 all-to-all-done
  124.0 5.8 %fusion.9 = f32[400,2048]{1,0:T(8,128)} fusion(bf16[1024,2048]{1,0:T(8,128)(2,1)} %all-gather.2.cloned.1.call-done, bf16[8,128,400]{1,2,0:T(8,128)(2,1)S(1)} %all-to-all-done), kind=kOutput, calls=%fused_computation.15 | convolution fusion | flops 1677721600 | bytes 8290304 | tf_op jit(solution)/shard_map/dot_general | solution.py:35
  (2 shorter events, 0.0 us)
Async XLA Ops:
  8.0 2.9 %copy-start = (bf16[128,2048]{1,0:T(8,128)(2,1)S(1)}, bf16[128,2048]{1,0:T(8,128)(2,1)}, u32[]{:S(2)}) copy-start(bf16[128,2048]{1,0:T(8,128)(2,1)} %param.10) | copy-start | bytes 1572868
  8.0 47.3 %reduce-scatter.2.cloned.1.call-start = ((), (), s32[]{:S(2)}) async-start(), calls=%async_computation.2 | async-start | bytes 1024000 | tf_op jit(solution)/shard_map/reduce_scatter | solution.py:32
  28.9 26.3 %copy-start.2 = (f32[3200]{0:T(1024)S(1)}, f32[3200]{0:T(1024)}, u32[]{:S(2)}) copy-start(f32[3200]{0:T(1024)} %param.7) | copy-start | bytes 38404
  28.9 69.2 %copy-start.1 = (bf16[32,3200]{1,0:T(8,128)(2,1)S(1)}, bf16[32,3200]{1,0:T(8,128)(2,1)}, u32[]{:S(2)}) copy-start(bf16[32,3200]{1,0:T(8,128)(2,1)} %param.11) | copy-start | bytes 614404
  29.0 91.6 %all-gather.2.cloned.1.call-start = ((), (), s32[]{:S(2)}) async-start(), calls=%async_computation.3 | async-start | bytes 4718592 | tf_op jit(solution)/shard_map/all_gather | solution.py:28
  30.8 93.1 %all-to-all-start = ((bf16[8,128,400]{1,2,0:T(8,128)(2,1)}), bf16[8,128,400]{1,2,0:T(8,128)(2,1)S(1)}, u32[]{:S(2)}, u32[]{:S(2)}) async-start(bf16[8,128,400]{1,2,0:T(8,128)(2,1)} %bitcast.1), calls=%async_computation.1 | async-start | bytes 1638400 | tf_op jit(solution)/shard_map/all_to_all | solution.py:19
Sparse Core Ops, SparseCore 0:
  29.1 26.1 reduce-scatter.1
Sparse Core Ops, SparseCore 1:
  31.6 88.9 all-gather.1
where the time goes:
time: 138 us; the launch traced here: 137 us
  blocking collectives  41.7 us (30%)
  waiting for transfers between devices  38.2 us (28%)
  matrix products  23.8 us (17%)
  between operations  15.5 us (11%)
  other arithmetic  9.2 us (7%)
  starting transfers between devices  7.39 us (5%)
  local copies, waits for them, and re-layouts  1.39 us (1%)
    psum x1, blocking collectives, on_device(): grad_gain = lax.psum(gain_part, ('dp', 'tensor'))  41.7 us
    all_gather x1, waiting for transfers between devices, on_device(): grad_pre_all = lax.all_gather(grad_pre, 'dp', axis=0, tiled=True)  20.6 us
    reduce_scatter x1, waiting for transfers between devices, on_device(): lax.psum_scatter(back_term.astype(jnp.bfloat16), 'tensor', scatter_dimens...  17 us
    dot_general x1, matrix products, on_device(): lax.dot_general(grad_pre, fc1_weight, (((1,), (1,)), ((), ())), preferred...  10 us
    dot_general x1, matrix products, on_device(): jnp.dot(normed, fc1_weight, preferred_element_type=jnp.float32) + fc1_bias  8 us
    all_to_all x1, starting transfers between devices, on_device(): lax.all_to_all(blocks, 'dp', 0, 0, tiled=True)  7.31 us
    dot_general x1, matrix products, on_device(): lax.dot_general(owned_cols, grad_pre_all, (((0,), (0,)), ((), ())), prefe...  5.75 us
    reduce_sum x1, other arithmetic, on_device(): grad_bias = jnp.sum(grad_pre_all.astype(jnp.float32), axis=0)  3.42 us
  transfers between devices with their start and end apart: 3, of which 2 were waited for; matrix products, arithmetic and copies ran while one was open for 6% of the time, Pallas kernels for 0%

commit v1 on v0

--- a/solution.py
+++ b/solution.py
@@ -4,6 +4,19 @@
 from jax.sharding import PartitionSpec as P
 
 epsilon = 1e-06
+
+
+def collect(x, axis, dim):
+    ways = lax.axis_size(axis)
+    up = [(d, (d + 1) % ways) for d in range(ways)]
+    down = [(d, (d - 1) % ways) for d in range(ways)]
+    earlier, later = ([x], [x])
+    for _ in range(ways // 2):
+        earlier.append(lax.ppermute(earlier[-1], axis, up))
+    for _ in range((ways - 1) // 2):
+        later.append(lax.ppermute(later[-1], axis, down))
+    line = jnp.concatenate([*earlier[::-1], *later[1:]], axis=dim)
+    return jnp.roll(line, (lax.axis_index(axis) - ways // 2) * x.shape[dim], axis=dim)
 
 
 def on_device(inputs, norm_gain, fc1_weight, fc1_bias, grad_act, grad_res):
@@ -25,7 +38,7 @@
         + preact * jnp.exp(-0.5 * preact * preact) * 0.3989422804014327
     )
     grad_pre = (grad_act.astype(jnp.float32) * derivative).astype(jnp.bfloat16)
-    grad_pre_all = lax.all_gather(grad_pre, "dp", axis=0, tiled=True)
+    grad_pre_all = collect(grad_pre, "dp", 0)
     back_term = lax.dot_general(
         grad_pre, fc1_weight, (((1,), (1,)), ((), ())), preferred_element_type=jnp.float32
     )

time: 138 us -> 191 us (1.38)
  waiting for transfers between devices: 38.2 us -> 57.4 us
  starting transfers between devices: 7.39 us -> 26.4 us
  local copies, waits for them, and re-layouts: 1.39 us -> 20.2 us
  matrix products: 23.8 us -> 18.7 us
    ppermute x0 -> x7, waiting for transfers between devices: none -> 57.4 us  [the longest x4 57.4 us: collect(): earlier.append(lax.ppermute(earlier[-1], axis, up))]
    ppermute x0 -> x7, starting transfers between devices: none -> 21.6 us  [the longest x3 10.9 us: collect(): later.append(lax.ppermute(later[-1], axis, down))]
    all_gather x1 -> x0, waiting for transfers between devices: 20.6 us -> none  [on_device(): grad_pre_all = lax.all_gather(grad_pre, 'dp', axis=0, tiled=True)]
    unnamed x6 -> x19, local copies, waits for them, and re-layouts: 0.01 us -> 18 us
    reduce_scatter x1, waiting for transfers between devices: 17 us -> 0.01 us  [on_device(): lax.psum_scatter(back_term.astype(jnp.bfloat16), 'tensor', scatter_dimens...]
    dot_general x1, matrix products: 10 us -> 5.22 us  [on_device(): lax.dot_general(grad_pre, fc1_weight, (((1,), (1,)), ((), ())), preferred...]
    all_to_all x1, starting transfers between devices: 7.31 us -> 4.78 us  [on_device(): lax.all_to_all(blocks, 'dp', 0, 0, tiled=True)]
  transfers between devices with their start and end apart: 3 -> 9, of which waited for: 2 -> 3; matrix products, arithmetic and copies ran while one was open for 6% -> 13% of each run, Pallas kernels for 0% -> 0%
where the time goes in v1:
time: 191 us; the launch traced here: 190 us
  waiting for transfers between devices  57.4 us (30%)
  blocking collectives  42.7 us (22%)
  starting transfers between devices  26.4 us (14%)
  local copies, waits for them, and re-layouts  20.2 us (11%)
  matrix products  18.7 us (10%)
  between operations  14.1 us (7%)
  other arithmetic  10.6 us (6%)
    ppermute x4, waiting for transfers between devices, collect(): earlier.append(lax.ppermute(earlier[-1], axis, up))  57.4 us
    psum x1, blocking collectives, on_device(): grad_gain = lax.psum(gain_part, ('dp', 'tensor'))  42.7 us
    unnamed x19, local copies, waits for them, and re-layouts  18 us
    ppermute x3, starting transfers between devices, collect(): later.append(lax.ppermute(later[-1], axis, down))  10.9 us
    ppermute x4, starting transfers between devices, collect(): earlier.append(lax.ppermute(earlier[-1], axis, up))  10.7 us
    dot_general x1, matrix products, on_device(): jnp.dot(normed, fc1_weight, preferred_element_type=jnp.float32) + fc1_bias  7.49 us
    dot_general x1, matrix products, on_device(): lax.dot_general(owned_cols, grad_pre_all, (((0,), (0,)), ((), ())), prefe...  6.01 us
    dot_general x1, matrix products, on_device(): lax.dot_general(grad_pre, fc1_weight, (((1,), (1,)), ((), ())), preferred...  5.22 us
  transfers between devices with their start and end apart: 9, of which 3 were waited for; matrix products, arithmetic and copies ran while one was open for 13% of the time, Pallas kernels for 0%

profile of v1, /device:TPU:0, one launch (start us, length us, event | category | flops | bytes accessed | tf_op | source)
XLA Modules:
  0.0 190.0 jit_solution(10142170630059102619)
XLA Ops:
  7.2 0.0 reduce-scatter.2.cloned.1.call-start
  7.2 1.4 fusion.2
  8.6 2.6 %convert_multiply_fusion = (f32[128,3200]{1,0:T(8,128)}, bf16[128,3200]{1,0:T(8,128)(2,1)S(1)}) fusion(bf16[128,3200]{1,0:T(8,128)(2,1)} %param.6, f32[128]{0:T(128)S(1)} %add_rsqrt_fusion, f32[3200]{0:T(1024)} %param.7), kind=kLoop, calls=%fused_computation.5 | loop fusion | flops 1638400 | bytes 3290112 | tf_op jit(solution)/shard_map/mul | solution.py:29
  11.2 0.0 copy-start
  11.2 7.5 %fusion.8 = bf16[128,2048]{1,0:T(8,128)(2,1)S(1)} fusion(bf16[128,3200]{1,0:T(8,128)(2,1)S(1)} %get-tuple-element.7, bf16[3200,2048]{1,0:T(8,128)(2,1)} %param.8, bf16[128,2048]{1,0:T(8,128)(2,1)} %param.10, f32[2048]{0:T(1024)} %param.9), kind=kOutput, calls=%fused_computation.15 | convolution fusion | flops 1680867328 | bytes 14983168 | tf_op jit(solution)/shard_map/dot_general | solution.py:35
  18.7 1.1 copy-done
  19.8 0.0 copy-start.1
  19.8 5.2 %convolution_convert_fusion = bf16[128,3200]{1,0:T(8,128)(2,1)} fusion(bf16[128,2048]{1,0:T(8,128)(2,1)S(1)} %fusion.8, bf16[3200,2048]{1,0:T(8,128)(2,1)S(1)} %copy-done), kind=kOutput, calls=%fused_computation.1 | convolution fusion | flops 1678131200 | bytes 14450688 | tf_op jit(solution)/shard_map/dot_general | solution.py:42
  25.0 0.0 reduce-scatter.2.cloned.1.call-update
  25.1 3.0 %collective-permute-start = (bf16[128,2048]{1,0:T(8,128)(2,1)S(1)}, bf16[128,2048]{1,0:T(8,128)(2,1)S(1)}, u32[]{:S(2)}, u32[]{:S(2)}) collective-permute-start(bf16[128,2048]{1,0:T(8,128)(2,1)S(1)} %fusion.8), channel_id=1, source_target_pairs={{0,4},{4,8},{8,12},{12,16},{16,20},{20,24},{24,28},{28,0},{1,5},{5... | collective-permute-start | bytes 1572872 | tf_op jit(solution)/shard_map/ppermute | solution.py:15
  28.1 3.1 %collective-permute-start.4 = (bf16[128,2048]{1,0:T(8,128)(2,1)S(1)}, bf16[128,2048]{1,0:T(8,128)(2,1)S(1)}, u32[]{:S(2)}, u32[]{:S(2)}) collective-permute-start(bf16[128,2048]{1,0:T(8,128)(2,1)S(1)} %fusion.8), channel_id=1, source_target_pairs={{0,28},{4,0},{8,4},{12,8},{16,12},{20,16},{24,20},{28,24},{1,29},{... | collective-permute-start | bytes 1572872 | tf_op jit(solution)/shard_map/ppermute | solution.py:17
  31.2 19.3 %collective-permute-done = bf16[128,2048]{1,0:T(8,128)(2,1)S(1)} collective-permute-done((bf16[128,2048]{1,0:T(8,128)(2,1)S(1)}, bf16[128,2048]{1,0:T(8,128)(2,1)S(1)}, u32[]{:S(2)}, u32[]{:S(2)}) %collective-permute-start) | collective-permute-done | bytes 524320 | tf_op jit(solution)/shard_map/ppermute | solution.py:15
  50.5 2.5 %collective-permute-start.1 = (bf16[128,2048]{1,0:T(8,128)(2,1)S(1)}, bf16[128,2048]{1,0:T(8,128)(2,1)}, u32[]{:S(2)}, u32[]{:S(2)}) collective-permute-start(bf16[128,2048]{1,0:T(8,128)(2,1)S(1)} %collective-permute-done), channel_id=1, source_target_pairs={{0,4},{4,8},{8,12},{12,16},{16,20},{20,24},{24,28},{28,0},{1,5},{5... | collective-permute-start | bytes 1572872 | tf_op jit(solution)/shard_map/ppermute | solution.py:15
  53.0 0.0 collective-permute-done.4
  53.0 3.0 %collective-permute-start.5 = (bf16[128,2048]{1,0:T(8,128)(2,1)S(1)}, bf16[128,2048]{1,0:T(8,128)(2,1)S(1)}, u32[]{:S(2)}, u32[]{:S(2)}) collective-permute-start(bf16[128,2048]{1,0:T(8,128)(2,1)S(1)} %collective-permute-done.4), channel_id=1, source_target_pairs={{0,28},{4,0},{8,4},{12,8},{16,12},{20,16},{24,20},{28,24},{1,29},{... | collective-permute-start | bytes 1572872 | tf_op jit(solution)/shard_map/ppermute | solution.py:17
  56.1 18.6 %collective-permute-done.1 = bf16[128,2048]{1,0:T(8,128)(2,1)} collective-permute-done((bf16[128,2048]{1,0:T(8,128)(2,1)S(1)}, bf16[128,2048]{1,0:T(8,128)(2,1)}, u32[]{:S(2)}, u32[]{:S(2)}) %collective-permute-start.1) | collective-permute-done | bytes 524320 | tf_op jit(solution)/shard_map/ppermute | solution.py:15
  74.7 2.6 %collective-permute-start.2 = (bf16[128,2048]{1,0:T(8,128)(2,1)}, bf16[128,2048]{1,0:T(8,128)(2,1)}, u32[]{:S(2)}, u32[]{:S(2)}) collective-permute-start(bf16[128,2048]{1,0:T(8,128)(2,1)} %collective-permute-done.1), channel_id=1, source_target_pairs={{0,4},{4,8},{8,12},{12,16},{16,20},{20,24},{24,28},{28,0},{1,5},{5... | collective-permute-start | bytes 1572872 | tf_op jit(solution)/shard_map/ppermute | solution.py:15
  77.3 1.3 copy.10
  78.5 4.8 %all-to-all-start = ((bf16[8,128,400]{1,2,0:T(8,128)(2,1)}), bf16[8,128,400]{1,2,0:T(8,128)(2,1)}, u32[]{:S(2)}, u32[]{:S(2)}) async-start(bf16[8,128,400]{1,2,0:T(8,128)(2,1)} %bitcast.1), calls=%async_computation.1 | async-start | bytes 1638400 | tf_op jit(solution)/shard_map/all_to_all | solution.py:32
  83.3 0.1 dynamic-slice.3
  83.4 0.0 collective-permute-done.5
  83.4 4.7 %collective-permute-start.6 = (bf16[128,2048]{1,0:T(8,128)(2,1)S(1)}, bf16[128,2048]{1,0:T(8,128)(2,1)S(1)}, u32[]{:S(2)}, u32[]{:S(2)}) collective-permute-start(bf16[128,2048]{1,0:T(8,128)(2,1)S(1)} %collective-permute-done.5), channel_id=1, source_target_pairs={{0,28},{4,0},{8,4},{12,8},{16,12},{20,16},{24,20},{28,24},{1,29},{... | collective-permute-start | bytes 1572872 | tf_op jit(solution)/shard_map/ppermute | solution.py:17
  88.1 19.5 %collective-permute-done.2 = bf16[128,2048]{1,0:T(8,128)(2,1)} collective-permute-done((bf16[128,2048]{1,0:T(8,128)(2,1)}, bf16[128,2048]{1,0:T(8,128)(2,1)}, u32[]{:S(2)}, u32[]{:S(2)}) %collective-permute-start.2) | collective-permute-done | bytes 524320 | tf_op jit(solution)/shard_map/ppermute | solution.py:15
  107.6 2.6 %collective-permute-start.3 = (bf16[128,2048]{1,0:T(8,128)(2,1)}, bf16[128,2048]{1,0:T(8,128)(2,1)S(1)}, u32[]{:S(2)}, u32[]{:S(2)}) collective-permute-start(bf16[128,2048]{1,0:T(8,128)(2,1)} %collective-permute-done.2), channel_id=1, source_target_pairs={{0,4},{4,8},{8,12},{12,16},{16,20},{20,24},{24,28},{28,0},{1,5},{5... | collective-permute-start | bytes 1572872 | tf_op jit(solution)/shard_map/ppermute | solution.py:15
  110.2 0.0 reduce-scatter.2.cloned.1.call-done
  110.2 1.3 fusion.17
  111.5 42.7 %psum.7 = f32[3200]{0:T(1024)} all-reduce(f32[3200]{0:T(1024)S(1)} %get-tuple-element.4), channel_id=1, replica_groups=mesh['dp'=8,'tensor'=4] {'dp','tensor'}, use_global_device_ids=true, to_apply=%region_5.6 | all-reduce | flops 3200 | bytes 25600 | tf_op jit(solution)/shard_map/psum | solution.py:62
  154.1 0.0 copy-done.1
  154.1 1.9 fusion.16
  156.0 0.0 collective-permute-done.3
  156.0 0.8 constant_dynamic-update-slice_fusion.15
  156.9 1.9 constant_dynamic-update-slice_fusion.14
  158.8 1.9 %constant_dynamic-update-slice_fusion.13 = bf16[2048,2048]{1,0:T(8,128)(2,1)} fusion(bf16[2048,2048]{1,0:T(8,128)(2,1)} %constant_dynamic-update-slice_fusion.14, bf16[128,2048]{1,0:T(8,128)(2,1)} %collective-permute-done.1), kind=kLoop, calls=%fused_computation.40 | loop fusion | bytes 1048576
  160.7 0.8 constant_dynamic-update-slice_fusion.12
  161.5 0.8 constant_dynamic-update-slice_fusion.11
  162.4 0.8 constant_dynamic-update-slice_fusion.10
  163.2 0.8 constant_dynamic-update-slice_fusion.9
  164.0 0.0 collective-permute-done.6
  164.0 0.8 constant_dynamic-update-slice_fusion.8
  164.9 0.8 constant_dynamic-update-slice_fusion.7
  165.7 1.9 %constant_dynamic-update-slice_fusion.6 = bf16[2048,2048]{1,0:T(8,128)(2,1)} fusion(bf16[2048,2048]{1,0:T(8,128)(2,1)} %constant_dynamic-update-slice_fusion.7, bf16[128,2048]{1,0:T(8,128)(2,1)} %collective-permute-done.2), kind=kLoop, calls=%fused_computation.33 | loop fusion | bytes 1048576
  167.6 1.9 constant_dynamic-update-slice_fusion.5
  169.5 0.8 constant_dynamic-update-slice_fusion.4
  170.4 0.9 constant_dynamic-update-slice_fusion.3
  171.2 0.9 constant_dynamic-update-slice_fusion.2
  172.1 0.8 constant_dynamic-update-slice_fusion.1
  172.9 0.8 constant_dynamic-update-slice_fusion
  173.7 3.4 %convert_reduce_fusion = f32[2048]{0:T(1024)} fusion(bf16[2048,2048]{1,0:T(8,128)(2,1)} %constant_dynamic-update-slice_fusion, s32[]{:T(128)S(6)} %select_n.19), kind=kLoop, calls=%fused_computation | loop fusion | flops 4192256 | bytes 4202500 | tf_op jit(solution)/shard_map/reduce_sum | solution.py:51
  177.2 0.0 all-to-all-done
  177.2 6.0 %fusion = f32[400,2048]{1,0:T(8,128)} fusion(bf16[2048,2048]{1,0:T(8,128)(2,1)} %constant_dynamic-update-slice_fusion, s32[]{:T(128)S(6)} %select_n.19, bf16[8,128,400]{1,2,0:T(8,128)(2,1)} %all-to-all-done), kind=kOutput, calls=%fused_computation.2 | convolution fusion | flops 1677721600 | bytes 8290308 | tf_op jit(solution)/shard_map/dot_general | solution.py:48
  (2 shorter events, 0.0 us)
Async XLA Ops:
  7.2 103.0 %reduce-scatter.2.cloned.1.call-start = ((), (), s32[]{:S(2)}) async-start(), calls=%async_computation.2 | async-start | bytes 1024000 | tf_op jit(solution)/shard_map/reduce_scatter | solution.py:45
  11.2 8.6 %copy-start = (bf16[3200,2048]{1,0:T(8,128)(2,1)S(1)}, bf16[3200,2048]{1,0:T(8,128)(2,1)}, u32[]{:S(2)}) copy-start(bf16[3200,2048]{1,0:T(8,128)(2,1)} %param.8) | copy-start | bytes 39321604
  19.8 134.3 %copy-start.1 = (bf16[32,3200]{1,0:T(8,128)(2,1)S(1)}, bf16[32,3200]{1,0:T(8,128)(2,1)}, u32[]{:S(2)}) copy-start(bf16[32,3200]{1,0:T(8,128)(2,1)} %param.11) | copy-start | bytes 614404
  25.1 25.5 %collective-permute-start = (bf16[128,2048]{1,0:T(8,128)(2,1)S(1)}, bf16[128,2048]{1,0:T(8,128)(2,1)S(1)}, u32[]{:S(2)}, u32[]{:S(2)}) collective-permute-start(bf16[128,2048]{1,0:T(8,128)(2,1)S(1)} %fusion.8), channel_id=1, source_target_pairs={{0,4},{4,8},{8,12},{12,16},{16,20},{20,24},{24,28},{28,0},{1,5},{5... | collective-permute-start | bytes 1572872 | tf_op jit(solution)/shard_map/ppermute | solution.py:15
  28.1 24.9 %collective-permute-start.4 = (bf16[128,2048]{1,0:T(8,128)(2,1)S(1)}, bf16[128,2048]{1,0:T(8,128)(2,1)S(1)}, u32[]{:S(2)}, u32[]{:S(2)}) collective-permute-start(bf16[128,2048]{1,0:T(8,128)(2,1)S(1)} %fusion.8), channel_id=1, source_target_pairs={{0,28},{4,0},{8,4},{12,8},{16,12},{20,16},{24,20},{28,24},{1,29},{... | collective-permute-start | bytes 1572872 | tf_op jit(solution)/shard_map/ppermute | solution.py:17
  50.5 24.1 %collective-permute-start.1 = (bf16[128,2048]{1,0:T(8,128)(2,1)S(1)}, bf16[128,2048]{1,0:T(8,128)(2,1)}, u32[]{:S(2)}, u32[]{:S(2)}) collective-permute-start(bf16[128,2048]{1,0:T(8,128)(2,1)S(1)} %collective-permute-done), channel_id=1, source_target_pairs={{0,4},{4,8},{8,12},{12,16},{16,20},{20,24},{24,28},{28,0},{1,5},{5... | collective-permute-start | bytes 1572872 | tf_op jit(solution)/shard_map/ppermute | solution.py:15
  53.0 30.4 %collective-permute-start.5 = (bf16[128,2048]{1,0:T(8,128)(2,1)S(1)}, bf16[128,2048]{1,0:T(8,128)(2,1)S(1)}, u32[]{:S(2)}, u32[]{:S(2)}) collective-permute-start(bf16[128,2048]{1,0:T(8,128)(2,1)S(1)} %collective-permute-done.4), channel_id=1, source_target_pairs={{0,28},{4,0},{8,4},{12,8},{16,12},{20,16},{24,20},{28,24},{1,29},{... | collective-permute-start | bytes 1572872 | tf_op jit(solution)/shard_map/ppermute | solution.py:17
  74.7 32.9 %collective-permute-start.2 = (bf16[128,2048]{1,0:T(8,128)(2,1)}, bf16[128,2048]{1,0:T(8,128)(2,1)}, u32[]{:S(2)}, u32[]{:S(2)}) collective-permute-start(bf16[128,2048]{1,0:T(8,128)(2,1)} %collective-permute-done.1), channel_id=1, source_target_pairs={{0,4},{4,8},{8,12},{12,16},{16,20},{20,24},{24,28},{28,0},{1,5},{5... | collective-permute-start | bytes 1572872 | tf_op jit(solution)/shard_map/ppermute | solution.py:15
  78.5 98.6 %all-to-all-start = ((bf16[8,128,400]{1,2,0:T(8,128)(2,1)}), bf16[8,128,400]{1,2,0:T(8,128)(2,1)}, u32[]{:S(2)}, u32[]{:S(2)}) async-start(bf16[8,128,400]{1,2,0:T(8,128)(2,1)} %bitcast.1), calls=%async_computation.1 | async-start | bytes 1638400 | tf_op jit(solution)/shard_map/all_to_all | solution.py:32
  83.4 80.6 %collective-permute-start.6 = (bf16[128,2048]{1,0:T(8,128)(2,1)S(1)}, bf16[128,2048]{1,0:T(8,128)(2,1)S(1)}, u32[]{:S(2)}, u32[]{:S(2)}) collective-permute-start(bf16[128,2048]{1,0:T(8,128)(2,1)S(1)} %collective-permute-done.5), channel_id=1, source_target_pairs={{0,28},{4,0},{8,4},{12,8},{16,12},{20,16},{24,20},{28,24},{1,29},{... | collective-permute-start | bytes 1572872 | tf_op jit(solution)/shard_map/ppermute | solution.py:17
  107.6 48.5 %collective-permute-start.3 = (bf16[128,2048]{1,0:T(8,128)(2,1)}, bf16[128,2048]{1,0:T(8,128)(2,1)S(1)}, u32[]{:S(2)}, u32[]{:S(2)}) collective-permute-start(bf16[128,2048]{1,0:T(8,128)(2,1)} %collective-permute-done.2), channel_id=1, source_target_pairs={{0,4},{4,8},{8,12},{12,16},{16,20},{20,24},{24,28},{28,0},{1,5},{5... | collective-permute-start | bytes 1572872 | tf_op jit(solution)/shard_map/ppermute | solution.py:15
Sparse Core Ops, SparseCore 0:
  25.2 26.1 reduce-scatter.1
